TPU v7x, 32 devices: a whole 2x2x4 slice. The times are simulated.
32 devices in a mesh: row: 2 (over x), col: 4 (over z), box: 4 (over y, core).
Axes of the slice: x: 2, y: 2, z: 4, core: 2. Of those that a mesh axis runs over, the one named last changes fastest.
Arguments:
- coeffs: bfloat16 [81920, 512], P(('row', 'box'), 'col'), may hold values from -6 to 6
- reflectors: bfloat16 [81920, 256], P(('row', 'box')), may hold values from -0.078125 to 0.078125
- factor: float32 [256, 256], replicated, may hold values from -0.375 to 0.375
- func_exp: float32 [81920], replicated, may hold values from 0.5 to 20
- func_atom: int32 [81920], replicated, may hold values from 0 to 8191, never falling along the last dimension, each value on 1 to 20 neighbouring positions
- atom_pos: float32 [3, 8192], replicated, may hold values from 0 to 1
- point_pos: float32 [3, 128, 128], P(None, ('row', 'col', 'box')), may hold values from 0 to 1
- send_tiles: int32 [8, 8, 2], replicated, may hold values from 0 to 79, as said below
- box_tiles: int32 [128, 16], P(('row', 'col', 'box')), may hold values from 0 to 15, as said below
- box_count: int32 [128], P(('row', 'col', 'box')), may hold values from 1 to 16
Outputs:
- rotated: bfloat16 [81920, 512], P(('row', 'box'), 'col')
- density: float32 [128, 128], P(('row', 'col', 'box'))
Inputs may be any that keep to these rules, and one draw needn't show every extreme that they name: `send_tiles`: for each basis group and box group the 2 tiles are different local tiles of the basis group. `box_tiles`: the 16 slots listed by a box are different. `func_atom`: never falls along the basis functions; every atom carries 1 to 20 functions.
All inputs are finite; a program needn't handle non-finite values.
Results may differ from a plain program's by a relative error of at most 0.015.
Values may be sent and summed in bfloat16 or wider, within the bound.
A program may use at most 128 MiB of HBM per device.

v0:
```python
import math
import jax
import jax.numpy as jnp
from jax import lax
from jax.sharding import PartitionSpec as P

K = 512
TILE = 128


def box_density(arrived, slot_alpha, slot_centre, listed, count, points):
    alpha = slot_alpha[listed]
    centre = slot_centre[:, listed]
    first = points[0][:, None, None] - centre[0][None]
    dist = first * first
    second = points[1][:, None, None] - centre[1][None]
    dist = dist + second * second
    third = points[2][:, None, None] - centre[2][None]
    dist = dist + third * third
    live = jnp.arange(listed.shape[0], dtype=jnp.int32) < count
    phi = jnp.where(live[None, :, None], jnp.exp(-alpha[None] * dist), 0.0).astype(jnp.bfloat16)
    phi = phi.reshape(points.shape[1], -1)
    block = arrived[listed].reshape(-1, arrived.shape[2])
    orbital = jnp.dot(phi, block, preferred_element_type=jnp.float32)
    return jnp.sum(orbital * orbital, 1) / (K * TILE)


def by_blocks(arrived, slot_alpha, slot_centre, lists, counts, points):
    boxes = lists.shape[0]
    width = math.gcd(boxes, 2)
    steps = boxes // width
    lists_blocked = lists.reshape(steps, width, lists.shape[1])
    counts_blocked = counts.reshape(steps, width)
    moved = jnp.moveaxis(points, 1, 0)
    points_blocked = moved.reshape(steps, width, moved.shape[1], moved.shape[2])
    single = jax.vmap(
        lambda listed, count, where: box_density(
            arrived, slot_alpha, slot_centre, listed, count, where
        )
    )

    def one_block(items):
        return single(items[0], items[1], items[2])

    result = lax.map(one_block, (lists_blocked, counts_blocked, points_blocked))
    return result.reshape(boxes, result.shape[2])


def per_device(
    coeffs,
    reflectors,
    factor,
    func_exp,
    func_atom,
    atom_pos,
    point_pos,
    send_tiles,
    box_tiles,
    box_count,
):
    panel_part = jnp.dot(reflectors.T, coeffs, preferred_element_type=jnp.float32)
    panel = lax.psum(panel_part.astype(jnp.bfloat16), ("row", "box")).astype(jnp.float32)
    scaled = jnp.dot(factor, panel, precision=lax.Precision.HIGHEST).astype(jnp.bfloat16)
    rotated = (
        coeffs.astype(jnp.float32) - jnp.dot(reflectors, scaled, preferred_element_type=jnp.float32)
    ).astype(jnp.bfloat16)
    peers = lax.axis_size(("row", "box"))
    group = lax.axis_index(("row", "box"))
    capacity = send_tiles.shape[2]
    local_tiles = coeffs.shape[0] // TILE
    slots = jnp.arange(peers * capacity, dtype=jnp.int32)
    source = slots // capacity
    within = slots % capacity
    tile = source * local_tiles + send_tiles[source, group, within]
    funcs = tile[:, None] * TILE + jnp.arange(TILE, dtype=jnp.int32)[None, :]
    slot_alpha = func_exp[funcs]
    slot_centre = atom_pos[:, func_atom[funcs]]
    outgoing_index = send_tiles[group]
    outgoing = rotated.reshape(local_tiles, TILE, rotated.shape[1])[outgoing_index]
    arrived = lax.all_to_all(outgoing, ("row", "box"), split_axis=0, concat_axis=0, tiled=True)
    arrived = arrived.reshape(peers * capacity, TILE, arrived.shape[3])
    lists, counts = (
        lax.all_gather(box_tiles, "col", axis=0, tiled=True),
        lax.all_gather(box_count, "col", axis=0, tiled=True),
    )
    points = lax.all_gather(point_pos, "col", axis=1, tiled=True)
    partial_value = by_blocks(arrived, slot_alpha, slot_centre, lists, counts, points)
    density = lax.psum_scatter(
        partial_value.astype(jnp.bfloat16), "col", scatter_dimension=0, tiled=True
    ).astype(jnp.float32)
    return (rotated, density)


def solution(mesh):
    in_specs = (
        P(("row", "box"), "col"),
        P(("row", "box"), None),
        P(),
        P(),
        P(),
        P(),
        P(None, ("row", "col", "box"), None),
        P(),
        P(("row", "col", "box"), None),
        P(("row", "col", "box")),
    )
    out_specs = (P(("row", "box"), "col"), P(("row", "col", "box"), None))
    return jax.shard_map(
        per_device, mesh=mesh, in_specs=in_specs, out_specs=out_specs, check_vma=False
    )
```

profile of v0, /device:TPU:0, one launch (start us, length us, event | category | flops | bytes accessed | tf_op | source)
XLA Modules:
  0.0 196.5 jit_solution(6431484893824231304)
XLA Ops:
  7.2 5.5 %convolution_convert_fusion = bf16[256,128]{1,0:T(8,128)(2,1)} fusion(bf16[10240,256]{1,0:T(8,128)(2,1)} %param.13, bf16[10240,128]{1,0:T(8,128)(2,1)} %param.12), kind=kOutput, calls=%fused_computation.42 | convolution fusion | flops 671121408 | bytes 7929856 | tf_op jit(solution)/shard_map/dot_general | solution.py:61
  13.8 3.0 %copy.28 = bf16[10240,128]{0,1:T(8,128)(2,1)S(1)} copy(bf16[10240,128]{1,0:T(8,128)(2,1)} %param.12) | data formatting | bytes 5242880 | tf_op args[0]
  16.8 2.6 %copy.31 = f32[3,8192]{0,1:T(8,128)} copy(f32[3,8192]{1,0:T(4,128)S(1)} %copy-done.5) | data formatting | bytes 196608 | tf_op args[5]
  19.4 48.7 %all-reduce.4.cloned.1.call-done = bf16[256,128]{1,0:T(8,128)(2,1)} async-done(((bf16[256,128]{1,0:T(8,128)(2,1)}), bf16[256,128]{1,0:T(8,128)(2,1)}) %all-reduce.4.cloned.1.call-update) | async-done | bytes 65552 | tf_op jit(solution)/shard_map/psum | solution.py:62
  69.3 5.8 %fusion.13 = bf16[10240,128]{0,1:T(8,128)(2,1)} fusion(bf16[128,256]{1,0:T(8,128)(2,1)S(1)} %convolution_convert_fusion.1, bf16[10240,256]{1,0:T(8,128)(2,1)} %param.13, bf16[10240,128]{0,1:T(8,128)(2,1)S(1)} %copy.28), kind=kOutput, calls=%fused_computation.41 | convolution fusion | flops 675020800 | bytes 10551296 | tf_op jit(solution)/shard_map/dot_general | solution.py:65
  75.1 3.2 %copy.36 = bf16[10240,128]{1,0:T(8,128)(2,1)S(1)} copy(bf16[10240,128]{0,1:T(8,128)(2,1)} %fusion.13) | data formatting | bytes 5242880
  78.3 1.6 gather_fusion.7
  80.0 3.5 %all-to-all-start = ((bf16[8,2,128,128]{3,2,1,0:T(8,128)(2,1)}), bf16[8,2,128,128]{3,2,1,0:T(8,128)(2,1)S(1)}, u32[]{:S(2)}, u32[]{:S(2)}) async-start(bf16[8,2,128,128]{3,2,1,0:T(8,128)(2,1)} %bitcast.116), calls=%async_computation | async-start | bytes 1048576 | tf_op jit(solution)/shard_map/all_to_all | solution.py:80
  83.6 11.8 %gather_fusion.5 = s32[2048]{0:T(1024)S(1)} fusion(s32[81920]{0:T(1024)S(1)} %copy-done, s32[2048]{0:T(1024)S(1)} %fusion.15), kind=kCustom, calls=%fused_computation.5 | custom fusion | bytes 24576 | tf_op jit(solution)/shard_map/gather | solution.py:77
  95.4 7.7 %gather_fusion.6 = f32[2048,3]{1,0:T(8,128)S(1)} fusion(f32[3,8192]{0,1:T(8,128)} %copy.31, s32[2048]{0:T(1024)S(1)} %fusion.17), kind=kCustom, calls=%fused_computation.6 | custom fusion | bytes 57344 | tf_op jit(solution)/shard_map/gather | solution.py:77
  103.4 11.8 %gather_fusion.4 = f32[2048]{0:T(1024)S(1)} fusion(f32[81920]{0:T(1024)S(1)} %copy-done.1, s32[2048]{0:T(1024)S(1)} %fusion.15), kind=kCustom, calls=%fused_computation.4 | custom fusion | bytes 24576 | tf_op jit(solution)/shard_map/gather | solution.py:76
  116.8 8.3 %all-reduce = s32[16]{0:T(128)S(1)} all-reduce(s32[16]{0:T(128)S(1)} %dynamic-update-slice), channel_id=1, replica_groups=mesh['row'=2,'col'=4,'box'=4] {'col'}, use_global_device_ids=true, to_apply=%add | all-reduce | flops 16 | bytes 128
  125.1 13.1 %all_gather.11 = f32[3,16,128]{2,0,1:T(4,128)S(1)} all-gather(f32[3,4,128]{2,0,1:T(4,128)S(1)} %copy.29), channel_id=1, replica_groups=mesh['row'=2,'col'=4,'box'=4] {'col'}, dimensions={1}, use_global_device_ids=true | all-gather | bytes 30720 | tf_op jit(solution)/shard_map/all_gather | solution.py:86
  138.9 11.9 %all-gather = s32[4,4,16]{2,1,0:T(4,128)S(1)} all-gather(s32[1,4,16]{2,1,0:T(4,128)S(1)} %bitcast.126), channel_id=1, replica_groups=mesh['row'=2,'col'=4,'box'=4] {'col'}, dimensions={0}, use_global_device_ids=true | all-gather | bytes 1280 | tf_op jit(solution)/shard_map/all_gather | solution.py:83
  150.8 29.7 %while.10 = (s32[]{:T(128)}, bf16[8,2,128]{2,1,0:T(2,128)(2,1)S(1)}, s32[8,2]{1,0:T(8,128)S(1)}, s32[8,2,16]{2,1,0:T(2,128)S(1)}, f32[16,128]{1,0:T(8,128)S(1)},...) while((s32[]{:T(128)}, ...), condition=%wide.region_3.4_spmd, body=%wide.region_1.3_spmd.sunk | while | flops 140055680 | bytes 3644613 | solution.py:45
  153.3 1.2 fusion.41
  157.0 1.2 fusion.41
  160.7 1.2 fusion.41
  164.4 1.2 fusion.41
  168.1 1.2 fusion.41
  171.8 1.2 fusion.41
  175.5 1.2 fusion.41
  179.3 1.2 fusion.41
  180.5 8.6 %all-reduce.1 = bf16[16,128]{1,0:T(8,128)(2,1)S(1)} all-reduce(bf16[16,128]{1,0:T(8,128)(2,1)S(1)} %bitcast.125), channel_id=2, replica_groups=mesh['row'=2,'col'=4,'box'=4] {'col'}, use_global_device_ids=true, to_apply=%region_4.5.clone | all-reduce | flops 2048 | bytes 8192
  (186 shorter events, 23.4 us)
Async XLA Ops:
  7.2 76.4 %copy-start = (s32[81920]{0:T(1024)S(1)}, s32[81920]{0:T(1024)}, u32[]{:S(2)}) copy-start(s32[81920]{0:T(1024)} %param.16) | copy-start | bytes 983044
  7.2 5.7 %copy-start.2 = (s32[8,8,2]{1,2,0:T(2,128)S(1)}, s32[8,8,2]{1,2,0:T(2,128)}, u32[]{:S(2)}) copy-start(s32[8,8,2]{1,2,0:T(2,128)} %param.19) | copy-start | bytes 1540
  7.2 60.9 %all-reduce.4.cloned.1.call-start = ((), (), s32[]{:S(2)}) async-start(), calls=%async_computation.1 | async-start | bytes 131072 | tf_op jit(solution)/shard_map/psum | solution.py:62
  13.7 3.1 %copy-start.5 = (f32[3,8192]{1,0:T(4,128)S(1)}, f32[3,8192]{1,0:T(4,128)}, u32[]{:S(2)}) copy-start(f32[3,8192]{1,0:T(4,128)} %param.17) | copy-start | bytes 294916
  16.8 51.3 %copy-start.4 = (f32[256,256]{1,0:T(8,128)S(1)}, f32[256,256]{1,0:T(8,128)}, u32[]{:S(2)}) copy-start(f32[256,256]{1,0:T(8,128)} %param.14) | copy-start | bytes 786436
  78.3 5.2 %copy-start.3 = (bf16[10240,128]{1,0:T(8,128)(2,1)}, bf16[10240,128]{1,0:T(8,128)(2,1)S(1)}, u32[]{:S(2)}) copy-start(bf16[10240,128]{1,0:T(8,128)(2,1)S(1)} %copy.36) | copy-start | bytes 7864324
  80.0 70.8 %all-to-all-start = ((bf16[8,2,128,128]{3,2,1,0:T(8,128)(2,1)}), bf16[8,2,128,128]{3,2,1,0:T(8,128)(2,1)S(1)}, u32[]{:S(2)}, u32[]{:S(2)}) async-start(bf16[8,2,128,128]{3,2,1,0:T(8,128)(2,1)} %bitcast.116), calls=%async_computation | async-start | bytes 1048576 | tf_op jit(solution)/shard_map/all_to_all | solution.py:80
  95.4 8.1 %copy-start.1 = (f32[81920]{0:T(1024)S(1)}, f32[81920]{0:T(1024)}, u32[]{:S(2)}) copy-start(f32[81920]{0:T(1024)} %param.15) | copy-start | bytes 983044
  103.4 11.8 %copy-start.8 = (u32[32]{0:T(128)S(1)}, u32[32]{0:T(128)}, u32[]{:S(2)}) copy-start(u32[32]{0:T(128)} %constant.107) | copy-start | bytes 388
  103.4 13.1 %copy-start.9 = (s32[4]{0:T(128)S(1)}, s32[4]{0:T(128)}, u32[]{:S(2)}) copy-start(s32[4]{0:T(128)} %param.21) | copy-start | bytes 52
  103.4 21.7 %copy-start.6 = (f32[3,4,128]{2,1,0:T(4,128)S(1)}, f32[3,4,128]{2,1,0:T(4,128)}, u32[]{:S(2)}) copy-start(f32[3,4,128]{2,1,0:T(4,128)} %param.18) | copy-start | bytes 18436
  103.4 35.5 %copy-start.7 = (s32[4,16]{1,0:T(4,128)S(1)}, s32[4,16]{1,0:T(4,128)}, u32[]{:S(2)}) copy-start(s32[4,16]{1,0:T(4,128)} %param.20) | copy-start | bytes 772
Sparse Core Ops, SparseCore 0:
  12.9 55.1 all-reduce.3
where the time goes:
time: 197 us
  local copies, waits for them, and re-layouts  62.4 us (32%)
  waiting for transfers between devices  48.7 us (25%)
  blocking collectives  41.9 us (21%)
  matrix products  22.2 us (11%)
  between operations  15.6 us (8%)
  starting transfers between devices  3.53 us (2%)
    psum x1, waiting for transfers between devices, per_device(): lax.psum(panel_part.astype(jnp.bfloat16), ('row', 'box'))  48.7 us
    gather x3, local copies, waits for them, and re-layouts, per_device(): slot_centre = atom_pos[:, func_atom[funcs]]  19.8 us
    unnamed x2, blocking collectives  16.9 us
    all_gather x1, blocking collectives, per_device(): points = lax.all_gather(point_pos, 'col', axis=1, tiled=True)  13.1 us
    all_gather x1, blocking collectives, per_device(): lax.all_gather(box_tiles, 'col', axis=0, tiled=True)  11.9 us
    gather x1, local copies, waits for them, and re-layouts, per_device(): slot_alpha = func_exp[funcs]  11.8 us
    unnamed x27, local copies, waits for them, and re-layouts  9.83 us
    dot_general x8, matrix products, box_density(): orbital = jnp.dot(phi, block, preferred_element_type=jnp.float32)  9.66 us
  transfers between devices with their start and end apart: 2, of which 1 were waited for; matrix products, arithmetic and copies ran while one was open for 20% of the time, Pallas kernels for 0%

commit v1 on v0

--- a/solution.py
+++ b/solution.py
@@ -59,7 +59,9 @@
     box_count,
 ):
     panel_part = jnp.dot(reflectors.T, coeffs, preferred_element_type=jnp.float32)
-    panel = lax.psum(panel_part.astype(jnp.bfloat16), ("row", "box")).astype(jnp.float32)
+    panel = jnp.sum(lax.all_gather(panel_part.astype(jnp.bfloat16), ("row", "box")), axis=0).astype(
+        jnp.float32
+    )
     scaled = jnp.dot(factor, panel, precision=lax.Precision.HIGHEST).astype(jnp.bfloat16)
     rotated = (
         coeffs.astype(jnp.float32) - jnp.dot(reflectors, scaled, preferred_element_type=jnp.float32)

time: 197 us -> 148 us (0.75)
  waiting for transfers between devices: 48.7 us -> 0.01 us
  between operations: 15.6 us -> 2.13 us
  blocking collectives: 41.9 us -> 53.5 us
    psum x1 -> x0, waiting for transfers between devices: 48.7 us -> none  [per_device(): lax.psum(panel_part.astype(jnp.bfloat16), ('row', 'box'))]
    all_gather x0 -> x1, blocking collectives: none -> 11.3 us  [per_device(): lax.all_gather(panel_part.astype(jnp.bfloat16), ('row', 'box'))]
    unnamed x27 -> x23, local copies, waits for them, and re-layouts: 9.83 us -> 10.6 us
  transfers between devices with their start and end apart: 2 -> 1, of which waited for: 1 -> 0; matrix products, arithmetic and copies ran while one was open for 20% -> 25% of each run, Pallas kernels for 0% -> 0%
where the time goes in v1:
time: 148 us; the launch traced here: 147 us
  local copies, waits for them, and re-layouts  63.2 us (43%)
  blocking collectives  53.5 us (36%)
  matrix products  21.7 us (15%)
  starting transfers between devices  3.49 us (2%)
  other arithmetic  2.39 us (2%)
  between operations  2.13 us (1%)
    gather x3, local copies, waits for them, and re-layouts, per_device(): slot_centre = atom_pos[:, func_atom[funcs]]  19.8 us
    unnamed x2, blocking collectives  17.2 us
    all_gather x1, blocking collectives, per_device(): points = lax.all_gather(point_pos, 'col', axis=1, tiled=True)  13.1 us
    all_gather x1, blocking collectives, per_device(): lax.all_gather(box_tiles, 'col', axis=0, tiled=True)  11.9 us
    gather x1, local copies, waits for them, and re-layouts, per_device(): slot_alpha = func_exp[funcs]  11.8 us
    all_gather x1, blocking collectives, per_device(): lax.all_gather(panel_part.astype(jnp.bfloat16), ('row', 'box'))  11.3 us
    unnamed x23, local copies, waits for them, and re-layouts  10.6 us
    dot_general x8, matrix products, box_density(): orbital = jnp.dot(phi, block, preferred_element_type=jnp.float32)  9.7 us
  transfers between devices with their start and end apart: 1, of which 0 were waited for; matrix products, arithmetic and copies ran while one was open for 25% of the time, Pallas kernels for 0%

profile of v1, /device:TPU:0, one launch (start us, length us, event | category | flops | bytes accessed | tf_op | source)
XLA Modules:
  0.0 147.1 jit_solution(17268729242324124420)
XLA Ops:
  1.6 3.0 %copy.28 = bf16[10240,128]{0,1:T(8,128)(2,1)S(1)} copy(bf16[10240,128]{1,0:T(8,128)(2,1)} %param.12) | data formatting | bytes 5242880 | tf_op args[0]
  4.5 4.9 %convolution_convert_fusion = bf16[256,128]{1,0:T(8,128)(2,1)S(1)} fusion(bf16[10240,256]{1,0:T(8,128)(2,1)} %param.13, bf16[10240,128]{1,0:T(8,128)(2,1)} %param.12), kind=kOutput, calls=%fused_computation.42 | convolution fusion | flops 671121408 | bytes 7929856 | tf_op jit(solution)/shard_map/dot_general | solution.py:61
  9.4 11.3 %all-gather = bf16[2048,128]{1,0:T(8,128)(2,1)S(1)} all-gather(bf16[256,128]{1,0:T(8,128)(2,1)S(1)} %convolution_convert_fusion), channel_id=2, replica_groups=mesh['row'=2,'col'=4,'box'=4] {'row','box'}, dimensions={0}, use_global_device_ids=true | all-gather | bytes 589824 | tf_op jit(solution)/shard_map/all_gather | solution.py:62
  20.8 1.2 convolution_convert_fusion.1
  22.1 5.9 %fusion.13 = bf16[10240,128]{0,1:T(8,128)(2,1)} fusion(bf16[128,256]{1,0:T(8,128)(2,1)S(1)} %convolution_convert_fusion.1, bf16[10240,256]{1,0:T(8,128)(2,1)} %param.13, bf16[10240,128]{0,1:T(8,128)(2,1)S(1)} %copy.28), kind=kOutput, calls=%fused_computation.41 | convolution fusion | flops 675020800 | bytes 10551296 | tf_op jit(solution)/shard_map/dot_general | solution.py:67
  27.9 3.2 %copy.36 = bf16[10240,128]{1,0:T(8,128)(2,1)S(1)} copy(bf16[10240,128]{0,1:T(8,128)(2,1)} %fusion.13) | data formatting | bytes 5242880
  31.2 1.6 %gather_fusion.7 = bf16[16,128,128]{2,1,0:T(8,128)(2,1)} fusion(bf16[80,128,128]{2,1,0:T(8,128)(2,1)S(1)} %bitcast.114, s32[1024]{0:T(1024)S(1)} %pad_clamp_fusion.1), kind=kCustom, calls=%fused_computation.7 | custom fusion | bytes 1048640 | tf_op jit(solution)/shard_map/gather | solution.py:81
  32.8 3.5 %all-to-all-start = ((bf16[8,2,128,128]{3,2,1,0:T(8,128)(2,1)}), bf16[8,2,128,128]{3,2,1,0:T(8,128)(2,1)S(1)}, u32[]{:S(2)}, u32[]{:S(2)}) async-start(bf16[8,2,128,128]{3,2,1,0:T(8,128)(2,1)} %bitcast.117), calls=%async_computation | async-start | bytes 1048576 | tf_op jit(solution)/shard_map/all_to_all | solution.py:82
  37.1 3.4 %copy.31 = f32[3,8192]{0,1:T(8,128)} copy(f32[3,8192]{1,0:T(4,128)} %param.17) | data formatting | bytes 196608 | tf_op args[5]
  40.6 11.8 %gather_fusion.5 = s32[2048]{0:T(1024)S(1)} fusion(s32[81920]{0:T(1024)S(1)} %copy-done, s32[2048]{0:T(1024)S(1)} %fusion.15), kind=kCustom, calls=%fused_computation.5 | custom fusion | bytes 24576 | tf_op jit(solution)/shard_map/gather | solution.py:79
  52.5 7.7 %gather_fusion.6 = f32[2048,3]{1,0:T(8,128)S(1)} fusion(f32[3,8192]{0,1:T(8,128)} %copy.31, s32[2048]{0:T(1024)S(1)} %fusion.17), kind=kCustom, calls=%fused_computation.6 | custom fusion | bytes 57344 | tf_op jit(solution)/shard_map/gather | solution.py:79
  60.5 11.8 %gather_fusion.4 = f32[2048]{0:T(1024)S(1)} fusion(f32[81920]{0:T(1024)S(1)} %copy-done.1, s32[2048]{0:T(1024)S(1)} %fusion.15), kind=kCustom, calls=%fused_computation.4 | custom fusion | bytes 24576 | tf_op jit(solution)/shard_map/gather | solution.py:78
  73.8 8.5 %all-reduce = s32[16]{0:T(128)S(1)} all-reduce(s32[16]{0:T(128)S(1)} %dynamic-update-slice), channel_id=1, replica_groups=mesh['row'=2,'col'=4,'box'=4] {'col'}, use_global_device_ids=true, to_apply=%add | all-reduce | flops 16 | bytes 128
  82.4 13.1 %all_gather.19 = f32[3,16,128]{2,0,1:T(4,128)S(1)} all-gather(f32[3,4,128]{2,0,1:T(4,128)S(1)} %copy.29), channel_id=1, replica_groups=mesh['row'=2,'col'=4,'box'=4] {'col'}, dimensions={1}, use_global_device_ids=true | all-gather | bytes 30720 | tf_op jit(solution)/shard_map/all_gather | solution.py:88
  96.2 11.9 %all-gather.1 = s32[4,4,16]{2,1,0:T(4,128)S(1)} all-gather(s32[1,4,16]{2,1,0:T(4,128)S(1)} %bitcast.128), channel_id=1, replica_groups=mesh['row'=2,'col'=4,'box'=4] {'col'}, dimensions={0}, use_global_device_ids=true | all-gather | bytes 1280 | tf_op jit(solution)/shard_map/all_gather | solution.py:85
  108.1 29.7 %while.10 = (s32[]{:T(128)}, bf16[8,2,128]{2,1,0:T(2,128)(2,1)S(1)}, s32[8,2]{1,0:T(8,128)S(1)}, s32[8,2,16]{2,1,0:T(2,128)S(1)}, f32[16,128]{1,0:T(8,128)S(1)},...) while((s32[]{:T(128)}, ...), condition=%wide.region_3.4_spmd, body=%wide.region_1.3_spmd.sunk | while | flops 140055680 | bytes 3644613 | solution.py:45
  110.6 1.2 fusion.41
  114.3 1.2 fusion.41
  118.0 1.2 fusion.41
  121.7 1.2 fusion.41
  125.4 1.2 fusion.41
  129.1 1.2 fusion.41
  132.9 1.2 fusion.41
  137.8 8.7 %all-reduce.1 = bf16[16,128]{1,0:T(8,128)(2,1)S(1)} all-reduce(bf16[16,128]{1,0:T(8,128)(2,1)S(1)} %bitcast.127), channel_id=3, replica_groups=mesh['row'=2,'col'=4,'box'=4] {'col'}, use_global_device_ids=true, to_apply=%region_4.5.clone | all-reduce | flops 2048 | bytes 8192
  (181 shorter events, 24.2 us)
Async XLA Ops:
  0.6 40.0 %copy-start = (s32[81920]{0:T(1024)S(1)}, s32[81920]{0:T(1024)}, u32[]{:S(2)}) copy-start(s32[81920]{0:T(1024)} %param.16) | copy-start | bytes 983044
  27.9 8.5 %copy-start.2 = (s32[8,8,2]{1,2,0:T(2,128)S(1)}, s32[8,8,2]{1,2,0:T(2,128)}, u32[]{:S(2)}) copy-start(s32[8,8,2]{1,2,0:T(2,128)} %param.19) | copy-start | bytes 1540
  31.2 9.4 %copy-start.3 = (bf16[10240,128]{1,0:T(8,128)(2,1)}, bf16[10240,128]{1,0:T(8,128)(2,1)S(1)}, u32[]{:S(2)}) copy-start(bf16[10240,128]{1,0:T(8,128)(2,1)S(1)} %copy.36) | copy-start | bytes 7864324
  32.8 75.2 %all-to-all-start = ((bf16[8,2,128,128]{3,2,1,0:T(8,128)(2,1)}), bf16[8,2,128,128]{3,2,1,0:T(8,128)(2,1)S(1)}, u32[]{:S(2)}, u32[]{:S(2)}) async-start(bf16[8,2,128,128]{3,2,1,0:T(8,128)(2,1)} %bitcast.117), calls=%async_computation | async-start | bytes 1048576 | tf_op jit(solution)/shard_map/all_to_all | solution.py:82
  52.4 8.1 %copy-start.1 = (f32[81920]{0:T(1024)S(1)}, f32[81920]{0:T(1024)}, u32[]{:S(2)}) copy-start(f32[81920]{0:T(1024)} %param.15) | copy-start | bytes 983044
  60.5 11.8 %copy-start.6 = (u32[32]{0:T(128)S(1)}, u32[32]{0:T(128)}, u32[]{:S(2)}) copy-start(u32[32]{0:T(128)} %constant.110) | copy-start | bytes 388
  60.5 13.1 %copy-start.7 = (s32[4]{0:T(128)S(1)}, s32[4]{0:T(128)}, u32[]{:S(2)}) copy-start(s32[4]{0:T(128)} %param.21) | copy-start | bytes 52
  60.5 21.9 %copy-start.4 = (f32[3,4,128]{2,1,0:T(4,128)S(1)}, f32[3,4,128]{2,1,0:T(4,128)}, u32[]{:S(2)}) copy-start(f32[3,4,128]{2,1,0:T(4,128)} %param.18) | copy-start | bytes 18436
  60.5 35.7 %copy-start.5 = (s32[4,16]{1,0:T(4,128)S(1)}, s32[4,16]{1,0:T(4,128)}, u32[]{:S(2)}) copy-start(s32[4,16]{1,0:T(4,128)} %param.20) | copy-start | bytes 772
